TPU v7x, 32 devices: a whole 2x2x4 slice. The times are simulated.
32 devices in a mesh: wide: 16 (over z, y, core), narrow: 2 (over x).
Axes of the slice: x: 2, y: 2, z: 4, core: 2. Of those that a mesh axis runs over, the one named last changes fastest.
Arguments:
- block_in: bfloat16 [32768, 768], P(('wide', 'narrow')), may hold values from -6 to 6
- out_grad: bfloat16 [32768, 768], P(('wide', 'narrow')), may hold values from -6 to 6
- seq_lens: int32 [16, 4], P('wide'), may hold values from 0 to 2048, as said below
- qkv_weight: bfloat16 [768, 2304], P(None, 'narrow'), may hold values from -0.21875 to 0.21875
- qkv_bias: bfloat16 [2304], P('narrow'), may hold values from -0.5 to 0.5
- out_weight: bfloat16 [768, 768], P('narrow'), may hold values from -0.875 to 0.875
- out_bias: bfloat16 [768], replicated, may hold values from -0.5 to 0.5
- up_weight: bfloat16 [768, 3072], P(None, 'narrow'), may hold values from -0.21875 to 0.21875
- up_bias: bfloat16 [3072], P('narrow'), may hold values from -0.5 to 0.5
- down_weight: bfloat16 [3072, 768], P('narrow'), may hold values from -0.109375 to 0.109375
- down_bias: bfloat16 [768], replicated, may hold values from -0.5 to 0.5
- attn_gain: bfloat16 [768], replicated, may hold values from 0.5 to 1.5
- attn_shift: bfloat16 [768], replicated, may hold values from -0.5 to 0.5
- ffn_gain: bfloat16 [768], replicated, may hold values from 0.5 to 1.5
- ffn_shift: bfloat16 [768], replicated, may hold values from -0.5 to 0.5
Outputs:
- block_out: bfloat16 [32768, 768], P(('wide', 'narrow'))
- in_grad: bfloat16 [32768, 768], P(('wide', 'narrow'))
- grad_qkv_weight: float32 [768, 2304], P(None, 'narrow')
- grad_qkv_bias: float32 [2304], P('narrow')
- grad_out_weight: float32 [768, 768], P('narrow')
- grad_out_bias: float32 [768], replicated
- grad_up_weight: float32 [768, 3072], P(None, 'narrow')
- grad_up_bias: float32 [3072], P('narrow')
- grad_down_weight: float32 [3072, 768], P('narrow')
- grad_down_bias: float32 [768], replicated
- grad_attn_gain: float32 [768], replicated
- grad_attn_shift: float32 [768], replicated
- grad_ffn_gain: float32 [768], replicated
- grad_ffn_shift: float32 [768], replicated
Inputs may be any that keep to these rules, and one draw needn't show every extreme that they name: `seq_lens`: each row is either 2048 followed by zeros or 512 in every slot; both kinds occur in every draw.
All inputs are finite; a program needn't handle non-finite values.
Results may differ from a plain program's by a relative error of at most 0.011.
Values may be sent and summed in bfloat16 or wider, within the bound.
No kernel may reach another device: no remote copies, remote signals or barrier semaphores. Data moves between devices by JAX's collectives and lax.ppermute only.
A program may use at most 256 MiB of HBM per device.

v0:
```python
import jax
import jax.numpy as jnp
from jax import lax
from jax.sharding import PartitionSpec as P

HD = 64
ROT = 16
EPS = 1e-05
NEG = -1e30
SCALE = 0.125


def norm_stats(rows):
    rows = rows.astype(jnp.float32)
    center = jnp.mean(rows, axis=-1, keepdims=True)
    offset = rows - center
    spread = jnp.mean(offset * offset, axis=-1, keepdims=True)
    inverse = lax.rsqrt(spread + EPS)
    return (offset * inverse, inverse)


def norm_back(grad_rows, normed, inverse, gain):
    scaled = grad_rows * gain.astype(jnp.float32)
    return inverse * (
        scaled
        - jnp.mean(scaled, axis=-1, keepdims=True)
        - normed * jnp.mean(scaled * normed, axis=-1, keepdims=True)
    )


def rotate(heads_rows, place, direction):
    half = ROT // 2
    freq = 1.0 / 10000.0 ** (jnp.arange(half, dtype=jnp.float32) * 2.0 / ROT)
    angle = place[:, None].astype(jnp.float32) * freq[None, :]
    cosine = jnp.cos(angle)[:, None, :]
    sine = jnp.sin(angle)[:, None, :] * direction
    first = heads_rows[..., :half]
    second = heads_rows[..., half:ROT]
    return jnp.concatenate(
        [first * cosine - second * sine, second * cosine + first * sine, heads_rows[..., ROT:]],
        axis=-1,
    )


def positions(lens_row, group_rows):
    ends = jnp.cumsum(lens_row)
    starts = ends - lens_row
    token_index = jnp.arange(group_rows, dtype=jnp.int32)
    segment = jnp.sum((token_index[:, None] >= ends[None, :]).astype(jnp.int32), axis=1)
    chosen = segment[:, None] == jnp.arange(lens_row.shape[0], dtype=jnp.int32)[None, :]
    begin = jnp.sum(jnp.where(chosen, starts[None, :], 0), axis=1)
    return (segment, token_index - begin)


def contract_rows(left, right):
    return lax.dot_general(
        left, right, (((0,), (0,)), ((), ())), preferred_element_type=jnp.float32
    )


def contract_cols(left, right):
    return lax.dot_general(
        left, right, (((1,), (1,)), ((), ())), preferred_element_type=jnp.float32
    )


def block_scores(query_rows, key_rows, segment, row_start):
    row_count = query_rows.shape[0]
    key_count = key_rows.shape[0]
    raw = (
        jnp.einsum("qhd,khd->hqk", query_rows, key_rows, preferred_element_type=jnp.float32) * SCALE
    )
    query_index = row_start + jnp.arange(row_count, dtype=jnp.int32)
    key_index = jnp.arange(key_count, dtype=jnp.int32)
    allowed = (
        segment[row_start : row_start + row_count][:, None] == segment[:key_count][None, :]
    ) & (key_index[None, :] <= query_index[:, None])
    return jnp.where(allowed[None], raw, NEG)


def per_device(
    block_in,
    out_grad,
    seq_lens,
    qkv_weight,
    qkv_bias,
    out_weight,
    out_bias,
    up_weight,
    up_bias,
    down_weight,
    down_bias,
    attn_gain,
    attn_shift,
    ffn_gain,
    ffn_shift,
):
    gathered = lax.all_gather(block_in, "narrow", axis=0, tiled=True)
    group_rows = gathered.shape[0]
    local_heads = qkv_weight.shape[1] // (3 * HD)
    segment, place = positions(seq_lens[0], group_rows)
    normed, inverse = norm_stats(gathered)
    first_in = (normed * attn_gain.astype(jnp.float32) + attn_shift.astype(jnp.float32)).astype(
        jnp.bfloat16
    )
    second_in = (normed * ffn_gain.astype(jnp.float32) + ffn_shift.astype(jnp.float32)).astype(
        jnp.bfloat16
    )
    packed = (
        jnp.dot(first_in, qkv_weight, preferred_element_type=jnp.float32)
        + qkv_bias.astype(jnp.float32)
    ).reshape(group_rows, local_heads, 3 * HD)
    queries = rotate(packed[..., :HD], place, 1.0).astype(jnp.bfloat16)
    keys_all = rotate(packed[..., HD : 2 * HD], place, 1.0).astype(jnp.bfloat16)
    values = packed[..., 2 * HD :].astype(jnp.bfloat16)
    hidden_pre = jnp.dot(second_in, up_weight, preferred_element_type=jnp.float32) + up_bias.astype(
        jnp.float32
    )
    activated = jax.nn.gelu(hidden_pre, approximate=False).astype(jnp.bfloat16)
    block_rows = min(512, group_rows)
    context_parts = []
    total_parts = []
    for row_start in range(0, group_rows, block_rows):
        row_stop = row_start + block_rows
        scores = block_scores(queries[row_start:row_stop], keys_all[:row_stop], segment, row_start)
        top = jnp.max(scores, axis=-1, keepdims=True)
        expo = jnp.exp(scores - top)
        row_total = jnp.sum(expo, axis=-1, keepdims=True)
        attn_probs = expo / row_total
        total_parts.append(top + jnp.log(row_total))
        context_parts.append(
            jnp.einsum(
                "hqk,khd->qhd",
                attn_probs.astype(jnp.bfloat16),
                values[:row_stop],
                preferred_element_type=jnp.float32,
            )
        )
    context = (
        jnp.concatenate(context_parts, axis=0)
        .reshape(group_rows, local_heads * HD)
        .astype(jnp.bfloat16)
    )
    partial_out = jnp.dot(context, out_weight, preferred_element_type=jnp.float32) + jnp.dot(
        activated, down_weight, preferred_element_type=jnp.float32
    )
    summed = lax.psum_scatter(partial_out, "narrow", scatter_dimension=0, tiled=True)
    block_out = (
        block_in.astype(jnp.float32)
        + summed
        + out_bias.astype(jnp.float32)
        + down_bias.astype(jnp.float32)
    ).astype(jnp.bfloat16)
    grad_rows = lax.all_gather(out_grad, "narrow", axis=0, tiled=True)
    bias_grad = jnp.sum(out_grad.astype(jnp.float32), axis=0)
    grad_out_w = contract_rows(context, grad_rows)
    grad_context = (
        contract_cols(grad_rows, out_weight)
        .astype(jnp.bfloat16)
        .reshape(group_rows, local_heads, HD)
    )
    grad_down_w = contract_rows(activated, grad_rows)
    grad_act = contract_cols(grad_rows, down_weight)
    _, gelu_back = jax.vjp(lambda value: jax.nn.gelu(value, approximate=False), hidden_pre)
    grad_hidden = gelu_back(grad_act)[0].astype(jnp.bfloat16)
    grad_up_w = contract_rows(second_in, grad_hidden)
    grad_up_b = jnp.sum(grad_hidden.astype(jnp.float32), axis=0)
    grad_second = contract_cols(grad_hidden, up_weight)
    query_parts = []
    grad_keys = jnp.zeros((group_rows, local_heads, HD), jnp.float32)
    grad_values = jnp.zeros((group_rows, local_heads, HD), jnp.float32)
    for part_index, row_start in enumerate(range(0, group_rows, block_rows)):
        row_stop = row_start + block_rows
        scores = block_scores(queries[row_start:row_stop], keys_all[:row_stop], segment, row_start)
        attn_probs = jnp.exp(scores - total_parts[part_index])
        grad_block = grad_context[row_start:row_stop]
        grad_values = grad_values.at[:row_stop].add(
            jnp.einsum(
                "hqk,qhd->khd",
                attn_probs.astype(jnp.bfloat16),
                grad_block,
                preferred_element_type=jnp.float32,
            )
        )
        grad_probs = jnp.einsum(
            "qhd,khd->hqk", grad_block, values[:row_stop], preferred_element_type=jnp.float32
        )
        weighted = jnp.sum(attn_probs * grad_probs, axis=-1, keepdims=True)
        grad_scores = (attn_probs * (grad_probs - weighted)).astype(jnp.bfloat16)
        query_parts.append(
            jnp.einsum(
                "hqk,khd->qhd", grad_scores, keys_all[:row_stop], preferred_element_type=jnp.float32
            )
            * SCALE
        )
        grad_keys = grad_keys.at[:row_stop].add(
            jnp.einsum(
                "hqk,qhd->khd",
                grad_scores,
                queries[row_start:row_stop],
                preferred_element_type=jnp.float32,
            )
            * SCALE
        )
    grad_queries = rotate(jnp.concatenate(query_parts, axis=0), place, -1.0)
    grad_keys = rotate(grad_keys, place, -1.0)
    grad_packed = (
        jnp.concatenate([grad_queries, grad_keys, grad_values], axis=-1)
        .reshape(group_rows, local_heads * 3 * HD)
        .astype(jnp.bfloat16)
    )
    grad_qkv_w = contract_rows(first_in, grad_packed)
    grad_qkv_b = jnp.sum(grad_packed.astype(jnp.float32), axis=0)
    grad_first = contract_cols(grad_packed, qkv_weight)
    grad_qkv_w, grad_qkv_b, grad_out_w, grad_up_w, grad_up_b, grad_down_w = lax.psum(
        (grad_qkv_w, grad_qkv_b, grad_out_w, grad_up_w, grad_up_b, grad_down_w), "wide"
    )
    first_share, second_share = (
        lax.psum_scatter(grad_first, "narrow", scatter_dimension=0, tiled=True),
        lax.psum_scatter(grad_second, "narrow", scatter_dimension=0, tiled=True),
    )
    own_normed, own_inverse = norm_stats(block_in)
    in_grad = (
        out_grad.astype(jnp.float32)
        + norm_back(first_share, own_normed, own_inverse, attn_gain)
        + norm_back(second_share, own_normed, own_inverse, ffn_gain)
    )
    vectors = (
        jnp.sum(first_share * own_normed, axis=0),
        jnp.sum(first_share, axis=0),
        jnp.sum(second_share * own_normed, axis=0),
        jnp.sum(second_share, axis=0),
        bias_grad,
    )
    attn_gain_g, attn_shift_g, ffn_gain_g, ffn_shift_g, bias_total = lax.psum(
        (vectors[0], vectors[1], vectors[2], vectors[3], vectors[4]), ("wide", "narrow")
    )
    return (
        block_out,
        in_grad.astype(jnp.bfloat16),
        grad_qkv_w,
        grad_qkv_b,
        grad_out_w,
        bias_total,
        grad_up_w,
        grad_up_b,
        grad_down_w,
        bias_total,
        attn_gain_g,
        attn_shift_g,
        ffn_gain_g,
        ffn_shift_g,
    )


def solution(mesh):
    placed = (
        P(("wide", "narrow"), None),
        P(("wide", "narrow"), None),
        P("wide", None),
        P(None, "narrow"),
        P("narrow"),
        P("narrow", None),
        P(),
        P(None, "narrow"),
        P("narrow"),
        P("narrow", None),
        P(),
        P(),
        P(),
        P(),
        P(),
    )
    return jax.shard_map(
        per_device,
        mesh=mesh,
        in_specs=placed,
        out_specs=(
            P(("wide", "narrow"), None),
            P(("wide", "narrow"), None),
            P(None, "narrow"),
            P("narrow"),
            P("narrow", None),
            P(),
            P(None, "narrow"),
            P("narrow"),
            P("narrow", None),
            P(),
            P(),
            P(),
            P(),
            P(),
        ),
        check_vma=False,
    )
```

profile of v0, /device:TPU:0, one launch (start us, length us, event | category | flops | bytes accessed | tf_op | source)
XLA Modules:
  0.0 851.6 jit_solution(16737983099656652931)
XLA Ops:
  13.5 1.4 fusion.79
  15.8 2.2 fusion.35
  17.9 1.7 fusion.62
  19.7 37.6 %all-gather.3.cloned.1.call-done = bf16[2048,768]{1,0:T(8,128)(2,1)} async-done(((bf16[1024,768]{1,0:T(8,128)(2,1)}), bf16[2048,768]{1,0:T(8,128)(2,1)}) %all-gather.3.cloned.1.call-update) | async-done | bytes 3145744 | tf_op jit(solution)/shard_map/all_gather | solution.py:98
  57.2 2.4 convert_reduce_fusion.2
  59.6 2.9 fusion.28
  62.6 41.1 %all-gather.5.cloned.1.call-done = bf16[2048,768]{1,0:T(8,128)(2,1)} async-done(((bf16[1024,768]{1,0:T(8,128)(2,1)}), bf16[2048,768]{1,0:T(8,128)(2,1)}) %all-gather.5.cloned.1.call-update) | async-done | bytes 3145744 | tf_op jit(solution)/shard_map/all_gather | solution.py:154
  103.8 3.5 convolution_convert_fusion
  108.4 7.1 convolution_add_fusion
  115.6 4.4 convert.35
  120.3 2.9 subtract_convert_fusion
  123.5 1.2 fusion.144
  126.9 4.1 multiply_reduce_fusion.3
  130.9 4.6 multiply_convert_fusion.4
  135.6 1.5 fusion.94
  138.9 3.4 fusion.143
  142.4 2.9 fusion.14
  145.3 8.0 multiply_reduce_fusion.2
  153.2 2.6 fusion.80
  155.9 1.7 copy-done.7
  157.5 6.2 multiply_convert_fusion.2
  163.7 3.0 fusion.93
  166.7 1.4 fusion.81
  168.1 8.3 fusion.142
  176.4 9.6 %fusion.2 = f32[6,512]{1,0:T(8,128)} fusion(f32[6,512,1536]{2,1,0:T(8,128)} %get-tuple-element.179, f32[6,512]{1,0:T(8,128)S(1)} %get-tuple-element.178), kind=kLoop, calls=%fused_computation.15 | loop fusion | flops 9434112 | bytes 18898944 | tf_op jit(solution)/shard_map/reduce_sum | solution.py:128
  186.8 13.2 %multiply_reduce_fusion.1 = (f32[6,512]{1,0:T(8,128)S(1)}, f32[6,512,1536]{2,1,0:T(8,128)}) fusion(f32[6,512,1536]{2,1,0:T(8,128)} %get-tuple-element.179, f32[6,512]{1,0:T(8,128)S(1)} %log_add_fusion.1, bf16[512,6,64]{0,2,1:T(8,128)(2,1)} %bitcast.112, bf16[2048,6,192]{0,2,1:T(8,128)(2,1)} %copy-done.11), kind=kOutput, calls=%fused_computation.10 | convolution fusion | flops 618132480 | bytes 39346176 | tf_op jit(solution)/shard_map/qhd,khd->hqk/dot_general | solution.py:185
  200.0 8.1 fusion.75
  208.1 1.6 copy-done.9
  209.7 13.0 %multiply_convert_fusion.1 = bf16[6,512,1536]{2,1,0:T(8,128)(2,1)S(1)} fusion(f32[6,512,1536]{2,1,0:T(8,128)} %get-tuple-element.181, f32[6,512,1536]{2,1,0:T(8,128)} %get-tuple-element.179, f32[6,512]{1,0:T(8,128)S(1)} %get-tuple-element.180, f32[6,512]{1,0:T(8,128)S(1)} %log_add_fusion.1), kind=kLoop, calls=%fused_computation.9 | loop fusion | flops 18874368 | bytes 47210496 | tf_op jit(solution)/shard_map/convert_element_type | solution.py:189
  222.8 3.8 fusion.92
  226.6 1.8 fusion.68
  228.5 10.7 %fusion.141 = (f32[6,512]{1,0:T(8,128)S(1)}, f32[6,512,2048]{2,1,0:T(8,128)}) fusion(bf16[2048,6,48]{0,2,1:T(8,128)(2,1)S(1)} %get-tuple-element.158, bf16[2048,6,8]{0,2,1:T(8,128)(2,1)S(1)} %copy-done.33, bf16[2048,6,8]{0,2,1:T(8,128)(2,1)S(1)} %copy-done.30, bf16[2048,6,64]{0,2,1:T(8,128)(2,1)S(1)} %copy-done.16, pred[512,2048]{1,0:T(8,128)(4,1)S(1)} %copy-done.42), kind=kOutput, calls=%fused_computation.222 | convolution fusion | flops 828896256 | bytes 28192768 | tf_op jit(solution)/shard_map/qhd,khd->hqk/dot_general | solution.py:71
  239.2 10.4 %fusion = f32[6,512]{1,0:T(8,128)S(1)} fusion(f32[6,512,2048]{2,1,0:T(8,128)} %get-tuple-element.175, f32[6,512]{1,0:T(8,128)S(1)} %get-tuple-element.174), kind=kLoop, calls=%fused_computation.6 | loop fusion | flops 12579840 | bytes 25190400 | tf_op jit(solution)/shard_map/reduce_sum | solution.py:128
  250.2 17.0 %multiply_reduce_fusion = (f32[6,512]{1,0:T(8,128)}, f32[6,512,2048]{2,1,0:T(8,128)}) fusion(f32[6,512,2048]{2,1,0:T(8,128)} %get-tuple-element.175, f32[6,512]{1,0:T(8,128)S(1)} %log_add_fusion, bf16[512,6,64]{0,2,1:T(8,128)(2,1)} %bitcast.110, bf16[2048,6,192]{0,2,1:T(8,128)(2,1)} %copy-done.11), kind=kOutput, calls=%fused_computation.1 | convolution fusion | flops 824177664 | bytes 52322304 | tf_op jit(solution)/shard_map/qhd,khd->hqk/dot_general | solution.py:185
  267.2 21.6 %multiply_convert_fusion = bf16[6,512,2048]{2,1,0:T(8,128)(2,1)} fusion(f32[6,512,2048]{2,1,0:T(8,128)} %get-tuple-element.177, f32[6,512,2048]{2,1,0:T(8,128)} %get-tuple-element.175, f32[6,512]{1,0:T(8,128)} %get-tuple-element.176, f32[6,512]{1,0:T(8,128)S(1)} %log_add_fusion), kind=kLoop, calls=%fused_computation | loop fusion | flops 25165824 | bytes 62939136 | tf_op jit(solution)/shard_map/convert_element_type | solution.py:189
  288.9 8.7 %fusion.91 = f32[512,6,64]{0,2,1:T(8,128)S(1)} fusion(bf16[6,512,2048]{2,1,0:T(8,128)(2,1)} %multiply_convert_fusion, bf16[2048,6,48]{0,2,1:T(8,128)(2,1)S(1)} %get-tuple-element.158, bf16[2048,6,8]{0,2,1:T(8,128)(2,1)S(1)} %copy-done.34, bf16[2048,6,8]{0,2,1:T(8,128)(2,1)S(1)} %copy-done.31), kind=kOutput, calls=%fused_computation.141 | convolution fusion | flops 810221568 | bytes 14942208 | tf_op jit(solution)/shard_map/hqk,khd->qhd/dot_general | solution.py:191
  297.6 7.1 bitcast_add_fusion.1
  310.1 12.0 %fusion.60 = bf16[2048,6,192]{0,2,1:T(8,128)(2,1)} fusion(bf16[2048,6,192]{0,2,1:T(8,128)(2,1)} %slice_dynamic-update-slice_fusion, f32[2048,6,64]{0,2,1:T(8,128)S(1)} %copy-done.10, bf16[512,6,64]{0,2,1:T(8,128)(2,1)S(1)} %bitcast.111, f32[6,512,2048]{2,1,0:T(8,128)} %get-tuple-element.175, f32[6,512]{1,0:T(8,128)S(1)} %log_add_fusion), kind=kOutput, calls=%fused_computation.104 | convolution fusion | flops 818675712 | bytes 31862784 | tf_op jit(solution)/shard_map/hqk,qhd->khd/dot_general | solution.py:178
  322.1 9.0 %fusion.146 = f32[2048,768]{1,0:T(8,128)} fusion(bf16[2048,1152]{0,1:T(8,128)(2,1)} %bitcast.26, bf16[768,1152]{1,0:T(8,128)(2,1)S(1)} %copy-done.84), kind=kOutput, calls=%fused_computation.227 | convolution fusion | flops 3623878656 | bytes 12779520 | tf_op jit(solution)/shard_map/dot_general | solution.py:62
  331.8 35.4 %multiply_convert_fusion.3 = (bf16[2048,1536]{1,0:T(8,128)(2,1)}, f32[2048,1536]{1,0:T(8,128)}, f32[2048,1536]{1,0:T(8,128)}) fusion(f32[1536]{0:T(1024)S(1)} %convert_element_type.145, bf16[768,1536]{1,0:T(8,128)(2,1)S(1)} %copy-done, bf16[2048,768]{1,0:T(8,128)(2,1)} %all-gather.3.cloned.1.call-done, f32[768]{0:T(1024)S(1)} %convert_element_type.143, ...), kind=kOutput, calls=%fused_computation.25 | convolution fusion | flops 5048893440 | bytes 36990976 | tf_op jit(solution)/shard_map/dot_general | solution.py:116
  367.2 16.0 %convert_reduce_fusion = (f32[1536]{0:T(1024)S(1)}, bf16[2048,1536]{1,0:T(8,128)(2,1)}) fusion(f32[2048,1536]{1,0:T(8,128)} %get-tuple-element.153, bf16[2048,768]{1,0:T(8,128)(2,1)S(1)} %copy-done.79, bf16[1536,768]{1,0:T(8,128)(2,1)S(1)} %copy-done.81, f32[2048,1536]{1,0:T(8,128)} %get-tuple-element.190, f32[1536]{0:T(1024)S(1)} %convert_element_type.145), kind=kOutput, calls=%fused_computation.19 | convolution fusion | flops 4885314048 | bytes 36974592 | tf_op jit(solution)/shard_map/dot_general | solution.py:62
  383.2 9.7 %fusion.147 = f32[2048,768]{1,0:T(8,128)} fusion(bf16[2048,1536]{1,0:T(8,128)(2,1)} %get-tuple-element.192, bf16[768,1536]{1,0:T(8,128)(2,1)S(1)} %copy-done), kind=kOutput, calls=%fused_computation.228 | convolution fusion | flops 4831838208 | bytes 14942208 | tf_op jit(solution)/shard_map/dot_general | solution.py:62
  393.7 4.3 fusion.106
  398.0 6.7 fusion.105
  406.3 5.4 fusion.104
  411.8 12.2 %fusion.101 = bf16[512,6,64]{0,2,1:T(8,128)(2,1)S(1)} fusion(f32[6,512,2048]{2,1,0:T(8,128)} %get-tuple-element.175, f32[6,512]{1,0:T(8,128)S(1)} %copy-done.60, f32[6,512]{1,0:T(8,128)S(1)} %copy-done.58, bf16[2048,6,192]{0,2,1:T(8,128)(2,1)} %copy-done.11), kind=kOutput, calls=%fused_computation.152 | convolution fusion | flops 824377344 | bytes 27156480 | tf_op jit(solution)/shard_map/hqk,khd->qhd/dot_general | solution.py:132
  424.2 7.7 fusion.145
  431.9 4.5 convolution_add_fusion.1
  436.5 5.1 fusion.148
  441.7 9.7 %fusion.134 = f32[768,1152]{1,0:T(8,128)} fusion(bf16[2048,1152]{0,1:T(8,128)(2,1)} %bitcast.26, bf16[2048,768]{1,0:T(8,128)(2,1)S(1)} %copy-done.18, f32[768]{0:T(1024)S(1)} %copy-done.71, f32[768]{0:T(1024)S(1)} %copy-done.62, f32[2048]{0:T(1024)S(1)} %copy-done.68, f32[2048]{0:T(1024)S(1)} %copy-done.66), kind=kOutput, calls=%fused_computation.218 | convolution fusion | flops 3633315840 | bytes 11425792 | tf_op jit(solution)/shard_map/dot_general | solution.py:56
  451.5 7.1 fusion.149
  458.6 7.2 fusion.130
  466.6 1.7 convert_reduce_fusion.3
  468.3 2.0 fusion.54
  470.3 3.1 convert_reduce_fusion.1
  473.5 61.1 %all-reduce.3 = (f32[1152]{0:T(1024)}, f32[1536]{0:T(1024)}) all-reduce(f32[1152]{0:T(1024)S(1)} %reduce_sum.246, f32[1536]{0:T(1024)S(1)} %get-tuple-element.191), channel_id=1, replica_groups=mesh['wide'=16,'narrow'=2] {'wide'}, use_global_device_ids=true, to_apply=%region_28.29 | all-reduce | flops 2688 | bytes 21504 | tf_op jit(solution)/shard_map/psum | solution.py:215
  534.5 4.7 fusion.52
  539.3 27.6 %reduce-scatter.4.cloned.1.call-done = f32[1024,768]{1,0:T(8,128)} async-done(((f32[2048,768]{1,0:T(8,128)}), f32[1024,768]{1,0:T(8,128)}) %reduce-scatter.4.cloned.1.call-update) | async-done | bytes 3145744 | tf_op jit(solution)/shard_map/reduce_scatter | solution.py:147
  566.9 6.9 convert_reduce_fusion.4
  573.8 41.8 %all-reduce.2 = (f32[768]{0:T(1024)S(1)}, f32[768]{0:T(1024)}, f32[768]{0:T(1024)}, f32[768]{0:T(1024)}, f32[768]{0:T(1024)}) all-reduce(f32[768]{0:T(1024)S(1)} %get-tuple-element.160, f32[768]{0:T(1024)S(1)} %get-tuple-element.128, f32[768]{0:T(1024)S(1)} %get-tuple-element.133, ...), channel_id=1, replica_groups=mesh['wide'=16,'narrow'=2] {'wide','narrow'}, use_global_device_ids=true, to_apply=%region_31.32 | all-reduce | flops 3840 | bytes 30720 | tf_op jit(solution)/shard_map/psum | solution.py:235
  615.6 217.2 %all-reduce.7.cloned.1.call-done = (f32[768,1152]{1,0:T(8,128)}, f32[384,768]{1,0:T(8,128)}, f32[768,1536]{1,0:T(8,128)}, f32[1536,768]{1,0:T(8,128)}) async-done(((f32[768,1152]{1,0:T(8,128)}, f32[384,768]{1,0:T(8,128)}, f32[768,1536]{1,0:T(8,128)}, f32[1536,768]{1,0:T(8,128)}), (f32[768,1152]{1,0:T(8,128)}, f32[384,768]{1,0:T(8,128)}, f32[768,1536]{1,0:T(8,128)}, ...) | async-done | bytes 14155792 | tf_op jit(solution)/shard_map/psum | solution.py:215
  833.4 4.3 copy.57
  838.8 2.4 copy.59
  842.3 2.2 copy.60
  (264 shorter events, 26.3 us)
Async XLA Ops:
  7.2 324.6 %copy-start = (bf16[768,1536]{1,0:T(8,128)(2,1)S(1)}, bf16[768,1536]{1,0:T(8,128)(2,1)}, u32[]{:S(2)}) copy-start(bf16[768,1536]{1,0:T(8,128)(2,1)} %param.42) | copy-start | bytes 7077892
  7.2 96.6 %copy-start.43 = (bf16[384,768]{1,0:T(8,128)(2,1)S(1)}, bf16[384,768]{1,0:T(8,128)(2,1)}, u32[]{:S(2)}) copy-start(bf16[384,768]{1,0:T(8,128)(2,1)} %param.40) | copy-start | bytes 1769476
  7.2 50.0 %all-gather.3.cloned.1.call-start = ((), (), s32[]{:S(2)}) async-start(), calls=%async_computation.3 | async-start | bytes 4718592 | tf_op jit(solution)/shard_map/all_gather | solution.py:98
  7.9 95.8 %all-gather.5.cloned.1.call-start = ((), (), s32[]{:S(2)}) async-start(), calls=%async_computation.5 | async-start | bytes 4718592 | tf_op jit(solution)/shard_map/all_gather | solution.py:154
  8.7 525.9 %reduce-scatter.6.cloned.1.call-start = ((), (), s32[]{:S(2)}) async-start(), calls=%async_computation.6 | async-start | bytes 9437184 | tf_op jit(solution)/shard_map/reduce_scatter | solution.py:219
  10.9 97.4 %copy-start.61 = (f32[768]{0:T(1024)}, f32[768]{0:T(1024)S(1)}, u32[]{:S(2)}) copy-start(f32[768]{0:T(1024)S(1)} %convert_element_type.131) | copy-start | bytes 9220
  11.6 96.8 %copy-start.70 = (f32[768]{0:T(1024)}, f32[768]{0:T(1024)S(1)}, u32[]{:S(2)}) copy-start(f32[768]{0:T(1024)S(1)} %convert_element_type.132) | copy-start | bytes 9220
  59.6 48.8 %copy-start.65 = (f32[2048]{0:T(1024)}, f32[2048]{0:T(1024)S(1)}, u32[]{:S(2)}) copy-start(f32[2048]{0:T(1024)S(1)} %broadcast_multiply_fusion.1) | copy-start | bytes 24580
  62.6 45.8 %copy-start.67 = (f32[2048]{0:T(1024)}, f32[2048]{0:T(1024)S(1)}, u32[]{:S(2)}) copy-start(f32[2048]{0:T(1024)S(1)} %add_rsqrt_fusion) | copy-start | bytes 24580
  120.0 6.8 copy-start.11
  123.5 13.6 %copy-start.14 = (bf16[2048,6,64]{0,2,1:T(8,128)(2,1)}, bf16[2048,6,64]{0,2,1:T(8,128)(2,1)S(1)}, u32[]{:S(2)}) copy-start(bf16[2048,6,64]{0,2,1:T(8,128)(2,1)S(1)} %get-tuple-element.193) | copy-start | bytes 4718596
  123.5 44.6 %copy-start.12 = (bf16[2048,6,64]{0,2,1:T(8,128)(2,1)}, bf16[2048,6,64]{0,2,1:T(8,128)(2,1)S(1)}, u32[]{:S(2)}) copy-start(bf16[2048,6,64]{0,2,1:T(8,128)(2,1)S(1)} %get-tuple-element.194) | copy-start | bytes 4718596
  124.8 6.1 copy-start.2
  125.7 5.2 copy-start.52
  142.3 15.2 %copy-start.1 = (f32[6,512,1024]{2,1,0:T(8,128)}, f32[6,512,1024]{2,1,0:T(8,128)S(1)}, u32[]{:S(2)}) copy-start(f32[6,512,1024]{2,1,0:T(8,128)S(1)} %get-tuple-element.183) | copy-start | bytes 37748740
  145.2 8.0 copy-start.54
  168.1 8.3 copy-start.3
  176.4 9.6 %copy-start.48 = (f32[6,512]{1,0:T(8,128)}, f32[6,512]{1,0:T(8,128)S(1)}, u32[]{:S(2)}) copy-start(f32[6,512]{1,0:T(8,128)S(1)} %get-tuple-element.178) | copy-start | bytes 36868
  186.8 13.2 %copy-start.8 = (f32[2048,6,64]{0,2,1:T(8,128)S(1)}, f32[2048,6,64]{0,2,1:T(8,128)}, u32[]{:S(2)}) copy-start(f32[2048,6,64]{0,2,1:T(8,128)} %copy-done.7) | copy-start | bytes 9437188
  186.8 13.2 %copy-start.24 = (bf16[512,384]{0,1:T(8,128)(2,1)S(1)}, bf16[512,384]{0,1:T(8,128)(2,1)}, u32[]{:S(2)}) copy-start(bf16[512,384]{0,1:T(8,128)(2,1)} %get-tuple-element.165) | copy-start | bytes 1179652
  209.7 13.0 %copy-start.13 = (bf16[2048,6,64]{0,2,1:T(8,128)(2,1)S(1)}, bf16[2048,6,64]{0,2,1:T(8,128)(2,1)}, u32[]{:S(2)}) copy-start(bf16[2048,6,64]{0,2,1:T(8,128)(2,1)} %copy-done.12) | copy-start | bytes 4718596
  228.4 10.7 %copy-start.5 = (f32[2048,6,64]{0,2,1:T(8,128)}, f32[2048,6,64]{0,2,1:T(8,128)S(1)}, u32[]{:S(2)}) copy-start(f32[2048,6,64]{0,2,1:T(8,128)S(1)} %fusion.68) | copy-start | bytes 9437188
  239.2 10.4 %copy-start.57 = (f32[6,512]{1,0:T(8,128)}, f32[6,512]{1,0:T(8,128)S(1)}, u32[]{:S(2)}) copy-start(f32[6,512]{1,0:T(8,128)S(1)} %get-tuple-element.174) | copy-start | bytes 36868
  267.2 21.6 %copy-start.31 = (bf16[2048,6,8]{0,2,1:T(8,128)(2,1)S(1)}, bf16[2048,6,8]{0,2,1:T(8,128)(2,1)}, u32[]{:S(2)}) copy-start(bf16[2048,6,8]{0,2,1:T(8,128)(2,1)} %copy-done.29) | copy-start | bytes 589828
  267.2 21.6 %copy-start.34 = (bf16[2048,6,8]{0,2,1:T(8,128)(2,1)S(1)}, bf16[2048,6,8]{0,2,1:T(8,128)(2,1)}, u32[]{:S(2)}) copy-start(bf16[2048,6,8]{0,2,1:T(8,128)(2,1)} %copy-done.32) | copy-start | bytes 589828
  288.9 8.7 %copy-start.6 = (f32[2048,6,64]{0,2,1:T(8,128)S(1)}, f32[2048,6,64]{0,2,1:T(8,128)}, u32[]{:S(2)}) copy-start(f32[2048,6,64]{0,2,1:T(8,128)} %copy-done.5) | copy-start | bytes 9437188
  297.5 7.2 copy-start.20
  297.5 7.2 copy-start.21
  297.5 7.2 copy-start.22
  297.6 7.2 copy-start.37
  297.6 7.2 copy-start.39
  310.1 12.0 %copy-start.84 = (bf16[768,1152]{1,0:T(8,128)(2,1)S(1)}, bf16[768,1152]{1,0:T(8,128)(2,1)}, u32[]{:S(2)}) copy-start(bf16[768,1152]{1,0:T(8,128)(2,1)} %param.38) | copy-start | bytes 5308420
  331.1 203.5 %reduce-scatter.8.cloned.1.call-start = ((), (), s32[]{:S(2)}) async-start(), calls=%async_computation.7 | async-start | bytes 9437184 | tf_op jit(solution)/shard_map/reduce_scatter | solution.py:220
  331.7 35.4 %copy-start.63 = (f32[768]{0:T(1024)}, f32[768]{0:T(1024)S(1)}, u32[]{:S(2)}) copy-start(f32[768]{0:T(1024)S(1)} %convert_element_type.142) | copy-start | bytes 9220
  331.7 35.4 %copy-start.72 = (f32[768]{0:T(1024)}, f32[768]{0:T(1024)S(1)}, u32[]{:S(2)}) copy-start(f32[768]{0:T(1024)S(1)} %convert_element_type.143) | copy-start | bytes 9220
  331.8 35.4 %copy-start.79 = (bf16[2048,768]{1,0:T(8,128)(2,1)S(1)}, bf16[2048,768]{1,0:T(8,128)(2,1)}, u32[]{:S(2)}) copy-start(bf16[2048,768]{1,0:T(8,128)(2,1)} %all-gather.5.cloned.1.call-done) | copy-start | bytes 9437188
  331.8 35.4 %copy-start.81 = (bf16[1536,768]{1,0:T(8,128)(2,1)S(1)}, bf16[1536,768]{1,0:T(8,128)(2,1)}, u32[]{:S(2)}) copy-start(bf16[1536,768]{1,0:T(8,128)(2,1)} %param.44) | copy-start | bytes 7077892
  393.0 173.8 %reduce-scatter.4.cloned.1.call-start = ((), (), s32[]{:S(2)}) async-start(), calls=%async_computation.4 | async-start | bytes 9437184 | tf_op jit(solution)/shard_map/reduce_scatter | solution.py:147
  393.7 11.0 %slice-start = ((s8[18874368]{0:T(1024)(128)(4,1)}), s8[4194304]{0:T(1024)(128)(4,1)S(1)}, s32[]{:S(2)}) async-start(s8[18874368]{0:T(1024)(128)(4,1)} %bitcast.100), calls=%async_computation.9 | async-start | bytes 8388608
  393.7 11.0 %slice-start.1 = ((s8[18874368]{0:T(1024)(128)(4,1)}), s8[4194304]{0:T(1024)(128)(4,1)S(1)}, s32[]{:S(2)}) async-start(s8[18874368]{0:T(1024)(128)(4,1)} %bitcast.100), calls=%async_computation.10 | async-start | bytes 8388608
  398.0 6.7 slice-start.2
  398.0 7.7 slice-start.3
  398.0 8.3 slice-start.4
  398.0 8.2 copy-start.49
  398.0 8.2 copy-start.56
  406.3 5.5 copy-start.58
  406.3 5.5 copy-start.60
  411.8 12.4 %copy-start.82 = (bf16[1536,768]{1,0:T(8,128)(2,1)S(1)}, bf16[1536,768]{1,0:T(8,128)(2,1)}, u32[]{:S(2)}) copy-start(bf16[1536,768]{1,0:T(8,128)(2,1)} %param.44) | copy-start | bytes 7077892
  424.1 7.7 copy-start.19
  424.1 7.7 copy-start.44
  436.4 5.3 copy-start.62
  436.4 5.3 copy-start.71
  436.4 396.4 %all-reduce.7.cloned.1.call-start = ((), (), s32[]{:S(2)}) async-start(), calls=%async_computation.8 | async-start | bytes 28311552 | tf_op jit(solution)/shard_map/psum | solution.py:215
  436.5 5.2 copy-start.18
  436.5 14.9 %slice-start.9 = ((s8[6291456]{0:T(1024)(128)(4,1)}), s8[4194304]{0:T(1024)(128)(4,1)S(1)}, s32[]{:S(2)}) async-start(s8[6291456]{0:T(1024)(128)(4,1)} %bitcast.121), calls=%async_computation.18 | async-start | bytes 8388608
  436.5 22.1 %slice-start.11 = ((s8[6291456]{0:T(1024)(128)(4,1)}), s8[4194304]{0:T(1024)(128)(4,1)S(1)}, s32[]{:S(2)}) async-start(s8[6291456]{0:T(1024)(128)(4,1)} %bitcast.123), calls=%async_computation.20 | async-start | bytes 8388608
  441.7 9.7 %copy-start.80 = (bf16[2048,768]{1,0:T(8,128)(2,1)S(1)}, bf16[2048,768]{1,0:T(8,128)(2,1)}, u32[]{:S(2)}) copy-start(bf16[2048,768]{1,0:T(8,128)(2,1)} %all-gather.5.cloned.1.call-done) | copy-start | bytes 9437188
  441.7 9.7 %slice-start.10 = ((s8[6291456]{0:T(1024)(128)(4,1)}), s8[2097152]{0:T(1024)(128)(4,1)S(1)}, s32[]{:S(2)}) async-start(s8[6291456]{0:T(1024)(128)(4,1)} %bitcast.121), calls=%async_computation.19 | async-start | bytes 4194304
  441.7 16.9 %slice-start.12 = ((s8[6291456]{0:T(1024)(128)(4,1)}), s8[2097152]{0:T(1024)(128)(4,1)S(1)}, s32[]{:S(2)}) async-start(s8[6291456]{0:T(1024)(128)(4,1)} %bitcast.123), calls=%async_computation.21 | async-start | bytes 4194304
  451.4 7.2 copy-start.64
  451.4 7.2 copy-start.73
  615.6 225.6 %copy-start.74 = (f32[768]{0:T(1024)}, f32[768]{0:T(1024)S(1)}, u32[]{:S(2)}) copy-start(f32[768]{0:T(1024)S(1)} %get-tuple-element.229) | copy-start | bytes 9220
  832.8 5.9 slice-start.7
  833.4 5.3 slice-start.8
  (40 other events, 102.8 us)
Sparse Core Ops, SparseCore 0:
  9.6 47.6 all-gather.2
  58.8 44.9 all-gather.4
  331.2 77.0 reduce-scatter.5
  410.5 77.0 reduce-scatter.7
  489.8 77.0 reduce-scatter.3
  573.1 259.6 all-reduce.6
where the time goes:
time: 859 us; the launch traced here: 852 us
  waiting for transfers between devices  325 us (38%)
  matrix products  269 us (31%)
  other arithmetic  116 us (14%)
  blocking collectives  103 us (12%)
  local copies, waits for them, and re-layouts  22.7 us (3%)
  between operations  15.6 us (2%)
    psum x1, waiting for transfers between devices, per_device(): lax.psum((grad_qkv_w, grad_qkv_b, grad_out_w, grad_up_w, grad_up_b, grad_...  217 us
    psum x1, blocking collectives, per_device(): lax.psum((grad_qkv_w, grad_qkv_b, grad_out_w, grad_up_w, grad_up_b, grad_...  61.1 us
    convert_element_type x4, other arithmetic, per_device(): grad_scores = (attn_probs * (grad_probs - weighted)).astype(jnp.bfloat16)  45.4 us
    dot_general x4, matrix products, per_device(): jnp.einsum('qhd,khd->hqk', grad_block, values[:row_stop], preferred_eleme...  42.3 us
    psum x1, blocking collectives, per_device(): lax.psum((vectors[0], vectors[1], vectors[2], vectors[3], vectors[4]), ('...  41.8 us
    all_gather x1, waiting for transfers between devices, per_device(): grad_rows = lax.all_gather(out_grad, 'narrow', axis=0, tiled=True)  41.1 us
    dot_general x4, matrix products, contract_cols(): lax.dot_general(left, right, (((1,), (1,)), ((), ())), preferred_element_...  38.2 us
    all_gather x1, waiting for transfers between devices, per_device(): gathered = lax.all_gather(block_in, 'narrow', axis=0, tiled=True)  37.6 us
  transfers between devices with their start and end apart: 6, of which 4 were waited for; matrix products, arithmetic and copies ran while one was open for 19% of the time, Pallas kernels for 0%

commit v1 on v0

--- a/solution.py
+++ b/solution.py
@@ -8,6 +8,18 @@
 EPS = 1e-05
 NEG = -1e30
 SCALE = 0.125
+
+
+def collect(shard, axis, dim):
+    ways, here, step = (lax.axis_size(axis), lax.axis_index(axis), shard.shape[dim])
+    line, have = (shard, 1)
+    while have < ways:
+        line = jnp.concatenate(
+            [line, lax.ppermute(line, axis, [(d, (d - have) % ways) for d in range(ways)])],
+            axis=dim,
+        )
+        have = 2 * have
+    return jnp.roll(line, here * step, axis=dim)
 
 
 def norm_stats(rows):
@@ -95,7 +107,7 @@
     ffn_gain,
     ffn_shift,
 ):
-    gathered = lax.all_gather(block_in, "narrow", axis=0, tiled=True)
+    gathered = collect(block_in, "narrow", 0)
     group_rows = gathered.shape[0]
     local_heads = qkv_weight.shape[1] // (3 * HD)
     segment, place = positions(seq_lens[0], group_rows)

time: 859 us -> 836 us (0.973)
  waiting for transfers between devices: 325 us -> 297 us
    ppermute x0 -> x1, waiting for transfers between devices: none -> 47.8 us  [collect(): lax.ppermute(line, axis, [(d, (d - have) % ways) for d in range(ways)])]
    all_gather x1, waiting for transfers between devices: 41.1 us -> 0.02 us  [per_device(): grad_rows = lax.all_gather(out_grad, 'narrow', axis=0, tiled=True)]
    all_gather x1 -> x0, waiting for transfers between devices: 37.6 us -> none  [per_device(): gathered = lax.all_gather(block_in, 'narrow', axis=0, tiled=True)]
    unnamed x202 -> x194, local copies, waits for them, and re-layouts: 20.5 us -> 22.4 us
  transfers between devices with their start and end apart: 6 -> 6, of which waited for: 4 -> 3; matrix products, arithmetic and copies ran while one was open for 19% -> 27% of each run, Pallas kernels for 0% -> 0%
where the time goes in v1:
time: 836 us; the launch traced here: 831 us
  waiting for transfers between devices  297 us (36%)
  matrix products  274 us (33%)
  other arithmetic  118 us (14%)
  blocking collectives  99.4 us (12%)
  local copies, waits for them, and re-layouts  24.3 us (3%)
  between operations  15.2 us (2%)
    psum x1, waiting for transfers between devices, per_device(): lax.psum((grad_qkv_w, grad_qkv_b, grad_out_w, grad_up_w, grad_up_b, grad_...  217 us
    psum x1, blocking collectives, per_device(): lax.psum((grad_qkv_w, grad_qkv_b, grad_out_w, grad_up_w, grad_up_b, grad_...  57.6 us
    convert_element_type x4, other arithmetic, per_device(): grad_scores = (attn_probs * (grad_probs - weighted)).astype(jnp.bfloat16)  48.8 us
    ppermute x1, waiting for transfers between devices, collect(): lax.ppermute(line, axis, [(d, (d - have) % ways) for d in range(ways)])  47.8 us
    psum x1, blocking collectives, per_device(): lax.psum((vectors[0], vectors[1], vectors[2], vectors[3], vectors[4]), ('...  41.8 us
    dot_general x4, matrix products, per_device(): jnp.einsum('qhd,khd->hqk', grad_block, values[:row_stop], preferred_eleme...  41.2 us
    dot_general x4, matrix products, contract_cols(): lax.dot_general(left, right, (((1,), (1,)), ((), ())), preferred_element_...  40.2 us
    dot_general x1, matrix products, per_device(): jnp.dot(second_in, up_weight, preferred_element_type=jnp.float32)  35.9 us
  transfers between devices with their start and end apart: 6, of which 3 were waited for; matrix products, arithmetic and copies ran while one was open for 27% of the time, Pallas kernels for 0%

profile of v1, /device:TPU:0, one launch (start us, length us, event | category | flops | bytes accessed | tf_op | source)
XLA Modules:
  0.0 831.1 jit_solution(14143859187600790800)
XLA Ops:
  8.0 3.0 collective-permute-start
  15.7 1.4 fusion.82
  18.1 2.2 fusion.35
  20.2 1.7 fusion.65
  21.9 47.8 %collective-permute-done = bf16[1024,768]{1,0:T(8,128)(2,1)} collective-permute-done((bf16[1024,768]{1,0:T(8,128)(2,1)}, bf16[1024,768]{1,0:T(8,128)(2,1)}, u32[]{:S(2)}, u32[]{:S(2)}) %collective-permute-start) | collective-permute-done | bytes 1572896 | tf_op jit(solution)/shard_map/ppermute | solution.py:18
  69.7 4.8 convert_reduce_fusion.2
  75.7 4.8 convolution_add_fusion
  82.1 1.5 copy-done.7
  85.9 1.3 log_add_fusion.3
  87.7 2.4 fusion.147
  90.1 3.1 fusion.14
  93.2 1.5 copy-done.1
  95.4 8.4 %fusion.146 = (f32[6,512]{1,0:T(8,128)S(1)}, f32[6,512,1536]{2,1,0:T(8,128)}) fusion(bf16[2048,6,64]{0,2,1:T(8,128)(2,1)S(1)} %get-tuple-element.196, bf16[2048,6,64]{0,2,1:T(8,128)(2,1)S(1)} %get-tuple-element.195, pred[512,1536]{1,0:T(8,128)(4,1)S(1)} %copy-done.26), kind=kOutput, calls=%fused_computation.230 | convolution fusion | flops 618132480 | bytes 21245952 | tf_op jit(solution)/shard_map/qhd,khd->hqk/dot_general | solution.py:83
  103.7 9.6 %fusion.2 = f32[6,512]{1,0:T(8,128)} fusion(f32[6,512,1536]{2,1,0:T(8,128)} %get-tuple-element.181, f32[6,512]{1,0:T(8,128)S(1)} %get-tuple-element.180), kind=kLoop, calls=%fused_computation.15 | loop fusion | flops 9434112 | bytes 18898944 | tf_op jit(solution)/shard_map/reduce_sum | solution.py:140
  114.7 11.9 %fusion.145 = (f32[6,512]{1,0:T(8,128)S(1)}, f32[6,512,2048]{2,1,0:T(8,128)}) fusion(bf16[2048,6,48]{0,2,1:T(8,128)(2,1)S(1)} %get-tuple-element.160, bf16[2048,6,8]{0,2,1:T(8,128)(2,1)} %copy-done.24, bf16[2048,6,8]{0,2,1:T(8,128)(2,1)} %copy-done.22, bf16[2048,6,64]{0,2,1:T(8,128)(2,1)} %copy-done.12, pred[512,2048]{1,0:T(8,128)(4,1)} %fusion.35), kind=kOutput, calls=%fused_computation.229 | convolution fusion | flops 828896256 | bytes 28192768 | tf_op jit(solution)/shard_map/qhd,khd->hqk/dot_general | solution.py:83
  126.6 10.9 %fusion = f32[6,512]{1,0:T(8,128)S(1)} fusion(f32[6,512,2048]{2,1,0:T(8,128)} %get-tuple-element.177, f32[6,512]{1,0:T(8,128)S(1)} %get-tuple-element.176), kind=kLoop, calls=%fused_computation.6 | loop fusion | flops 12579840 | bytes 25190400 | tf_op jit(solution)/shard_map/reduce_sum | solution.py:140
  138.1 3.5 convolution_convert_fusion
  142.5 3.9 fusion.90
  146.4 5.0 multiply_reduce_fusion.3
  151.4 6.4 multiply_convert_fusion.4
  157.8 3.4 fusion.97
  161.2 3.2 fusion.93
  165.2 7.4 multiply_reduce_fusion.2
  172.7 2.6 fusion.83
  175.3 6.5 multiply_convert_fusion.2
  181.8 2.9 fusion.96
  184.8 1.4 fusion.84
  186.2 12.5 %multiply_reduce_fusion.1 = (f32[6,512]{1,0:T(8,128)S(1)}, f32[6,512,1536]{2,1,0:T(8,128)}) fusion(f32[6,512,1536]{2,1,0:T(8,128)} %get-tuple-element.181, f32[6,512]{1,0:T(8,128)S(1)} %copy-done.35, bf16[512,6,64]{0,2,1:T(8,128)(2,1)S(1)} %bitcast.116, bf16[2048,6,192]{0,2,1:T(8,128)(2,1)} %copy-done.7), kind=kOutput, calls=%fused_computation.10 | convolution fusion | flops 618132480 | bytes 39346176 | tf_op jit(solution)/shard_map/qhd,khd->hqk/dot_general | solution.py:197
  198.8 8.1 fusion.78
  206.9 14.0 %multiply_convert_fusion.1 = bf16[6,512,1536]{2,1,0:T(8,128)(2,1)S(1)} fusion(f32[6,512,1536]{2,1,0:T(8,128)} %get-tuple-element.183, f32[6,512,1536]{2,1,0:T(8,128)} %get-tuple-element.181, f32[6,512]{1,0:T(8,128)S(1)} %get-tuple-element.182, f32[6,512]{1,0:T(8,128)S(1)} %copy-done.35), kind=kLoop, calls=%fused_computation.9 | loop fusion | flops 18874368 | bytes 47210496 | tf_op jit(solution)/shard_map/convert_element_type | solution.py:201
  220.9 2.9 fusion.95
  223.9 1.8 fusion.71
  225.7 1.7 copy-done.3
  227.3 16.3 %multiply_reduce_fusion = (f32[6,512]{1,0:T(8,128)S(1)}, f32[6,512,2048]{2,1,0:T(8,128)}) fusion(f32[6,512,2048]{2,1,0:T(8,128)} %get-tuple-element.177, f32[6,512]{1,0:T(8,128)S(1)} %log_add_fusion, bf16[512,6,64]{0,2,1:T(8,128)(2,1)} %bitcast.114, bf16[2048,6,192]{0,2,1:T(8,128)(2,1)} %copy-done.7), kind=kOutput, calls=%fused_computation.1 | convolution fusion | flops 824177664 | bytes 52322304 | tf_op jit(solution)/shard_map/qhd,khd->hqk/dot_general | solution.py:197
  243.6 21.9 %multiply_convert_fusion = bf16[6,512,2048]{2,1,0:T(8,128)(2,1)} fusion(f32[6,512,2048]{2,1,0:T(8,128)} %get-tuple-element.179, f32[6,512,2048]{2,1,0:T(8,128)} %get-tuple-element.177, f32[6,512]{1,0:T(8,128)S(1)} %get-tuple-element.178, f32[6,512]{1,0:T(8,128)S(1)} %log_add_fusion), kind=kLoop, calls=%fused_computation | loop fusion | flops 25165824 | bytes 62939136 | tf_op jit(solution)/shard_map/convert_element_type | solution.py:201
  265.5 8.7 %fusion.94 = f32[512,6,64]{0,2,1:T(8,128)S(1)} fusion(bf16[6,512,2048]{2,1,0:T(8,128)(2,1)} %multiply_convert_fusion, bf16[2048,6,48]{0,2,1:T(8,128)(2,1)S(1)} %copy-done.11, bf16[2048,6,8]{0,2,1:T(8,128)(2,1)S(1)} %copy-done.25, bf16[2048,6,8]{0,2,1:T(8,128)(2,1)S(1)} %copy-done.23), kind=kOutput, calls=%fused_computation.148 | convolution fusion | flops 810221568 | bytes 14942208 | tf_op jit(solution)/shard_map/hqk,khd->qhd/dot_general | solution.py:203
  274.2 7.1 bitcast_add_fusion.1
  286.7 11.8 %fusion.63 = bf16[2048,6,192]{0,2,1:T(8,128)(2,1)} fusion(bf16[2048,6,192]{0,2,1:T(8,128)(2,1)} %slice_dynamic-update-slice_fusion, f32[2048,6,64]{0,2,1:T(8,128)S(1)} %copy-done.6, bf16[512,6,64]{0,2,1:T(8,128)(2,1)S(1)} %bitcast.115, f32[6,512,2048]{2,1,0:T(8,128)} %get-tuple-element.177, f32[6,512]{1,0:T(8,128)S(1)} %log_add_fusion), kind=kOutput, calls=%fused_computation.111 | convolution fusion | flops 818675712 | bytes 31862784 | tf_op jit(solution)/shard_map/hqk,qhd->khd/dot_general | solution.py:190
  298.5 9.8 %fusion.150 = f32[2048,768]{1,0:T(8,128)} fusion(bf16[2048,1152]{0,1:T(8,128)(2,1)} %bitcast.26, bf16[768,1152]{1,0:T(8,128)(2,1)} %param.38), kind=kOutput, calls=%fused_computation.234 | convolution fusion | flops 3623878656 | bytes 12779520 | tf_op jit(solution)/shard_map/dot_general | solution.py:74
  309.1 35.9 %multiply_convert_fusion.3 = (bf16[2048,1536]{1,0:T(8,128)(2,1)}, f32[2048,1536]{1,0:T(8,128)}, f32[2048,1536]{1,0:T(8,128)}) fusion(f32[1536]{0:T(1024)S(1)} %convert_element_type.145, bf16[768,1536]{1,0:T(8,128)(2,1)S(1)} %copy-done, bf16[2048,768]{1,0:T(8,128)(2,1)} %copy-done.14, f32[768]{0:T(1024)S(1)} %convert_element_type.143, ...), kind=kOutput, calls=%fused_computation.25 | convolution fusion | flops 5048893440 | bytes 36990976 | tf_op jit(solution)/shard_map/dot_general | solution.py:128
  345.1 17.1 %convert_reduce_fusion = (f32[1536]{0:T(1024)S(1)}, bf16[2048,1536]{1,0:T(8,128)(2,1)}) fusion(f32[2048,1536]{1,0:T(8,128)} %get-tuple-element.153, bf16[2048,768]{1,0:T(8,128)(2,1)S(1)} %copy-done.71, bf16[1536,768]{1,0:T(8,128)(2,1)S(1)} %copy-done.73, f32[2048,1536]{1,0:T(8,128)} %get-tuple-element.192, f32[1536]{0:T(1024)S(1)} %convert_element_type.145), kind=kOutput, calls=%fused_computation.19 | convolution fusion | flops 4885314048 | bytes 36974592 | tf_op jit(solution)/shard_map/dot_general | solution.py:74
  362.2 9.8 %fusion.151 = f32[2048,768]{1,0:T(8,128)} fusion(bf16[2048,1536]{1,0:T(8,128)(2,1)} %get-tuple-element.194, bf16[768,1536]{1,0:T(8,128)(2,1)S(1)} %copy-done), kind=kOutput, calls=%fused_computation.235 | convolution fusion | flops 4831838208 | bytes 14942208 | tf_op jit(solution)/shard_map/dot_general | solution.py:74
  372.7 4.3 fusion.109
  377.0 6.7 fusion.108
  385.3 5.4 fusion.107
  390.8 12.2 %fusion.104 = bf16[512,6,64]{0,2,1:T(8,128)(2,1)S(1)} fusion(f32[6,512,2048]{2,1,0:T(8,128)} %get-tuple-element.177, f32[6,512]{1,0:T(8,128)S(1)} %copy-done.52, f32[6,512]{1,0:T(8,128)S(1)} %copy-done.50, bf16[2048,6,192]{0,2,1:T(8,128)(2,1)} %copy-done.7), kind=kOutput, calls=%fused_computation.159 | convolution fusion | flops 824377344 | bytes 27156480 | tf_op jit(solution)/shard_map/hqk,khd->qhd/dot_general | solution.py:144
  403.2 7.7 fusion.149
  410.9 4.5 convolution_add_fusion.1
  415.5 5.3 fusion.152
  420.8 9.7 %fusion.137 = f32[768,1152]{1,0:T(8,128)} fusion(bf16[2048,1152]{0,1:T(8,128)(2,1)} %bitcast.26, bf16[2048,768]{1,0:T(8,128)(2,1)S(1)} %copy-done.15, f32[768]{0:T(1024)S(1)} %copy-done.63, f32[768]{0:T(1024)S(1)} %copy-done.54, f32[2048]{0:T(1024)S(1)} %copy-done.60, f32[2048]{0:T(1024)S(1)} %copy-done.58), kind=kOutput, calls=%fused_computation.225 | convolution fusion | flops 3633315840 | bytes 11425792 | tf_op jit(solution)/shard_map/dot_general | solution.py:68
  430.5 7.1 fusion.153
  437.7 7.2 fusion.133
  445.6 1.7 convert_reduce_fusion.3
  447.3 2.0 fusion.54
  449.4 3.2 convert_reduce_fusion.1
  452.6 57.6 %all-reduce.3 = (f32[1152]{0:T(1024)}, f32[1536]{0:T(1024)}) all-reduce(f32[1152]{0:T(1024)S(1)} %reduce_sum.246, f32[1536]{0:T(1024)S(1)} %get-tuple-element.193), channel_id=1, replica_groups=mesh['wide'=16,'narrow'=2] {'wide'}, use_global_device_ids=true, to_apply=%region_28.29 | all-reduce | flops 2688 | bytes 21504 | tf_op jit(solution)/shard_map/psum | solution.py:227
  510.2 4.8 fusion.52
  515.0 31.7 %reduce-scatter.4.cloned.1.call-done = f32[1024,768]{1,0:T(8,128)} async-done(((f32[2048,768]{1,0:T(8,128)}), f32[1024,768]{1,0:T(8,128)}) %reduce-scatter.4.cloned.1.call-update) | async-done | bytes 3145744 | tf_op jit(solution)/shard_map/reduce_scatter | solution.py:159
  546.7 6.9 convert_reduce_fusion.4
  553.6 41.8 %all-reduce.2 = (f32[768]{0:T(1024)S(1)}, f32[768]{0:T(1024)}, f32[768]{0:T(1024)}, f32[768]{0:T(1024)}, f32[768]{0:T(1024)}) all-reduce(f32[768]{0:T(1024)S(1)} %get-tuple-element.162, f32[768]{0:T(1024)S(1)} %get-tuple-element.128, f32[768]{0:T(1024)S(1)} %get-tuple-element.133, ...), channel_id=1, replica_groups=mesh['wide'=16,'narrow'=2] {'wide','narrow'}, use_global_device_ids=true, to_apply=%region_31.32 | all-reduce | flops 3840 | bytes 30720 | tf_op jit(solution)/shard_map/psum | solution.py:247
  595.4 217.2 %all-reduce.7.cloned.1.call-done = (f32[768,1152]{1,0:T(8,128)}, f32[384,768]{1,0:T(8,128)}, f32[768,1536]{1,0:T(8,128)}, f32[1536,768]{1,0:T(8,128)}) async-done(((f32[768,1152]{1,0:T(8,128)}, f32[384,768]{1,0:T(8,128)}, f32[768,1536]{1,0:T(8,128)}, f32[1536,768]{1,0:T(8,128)}), (f32[768,1152]{1,0:T(8,128)}, f32[384,768]{1,0:T(8,128)}, f32[768,1536]{1,0:T(8,128)}, ...) | async-done | bytes 14155792 | tf_op jit(solution)/shard_map/psum | solution.py:227
  813.2 4.3 copy.57
  818.6 2.4 copy.59
  822.1 2.2 copy.60
  (257 shorter events, 28.1 us)
Async XLA Ops:
  7.2 301.9 %copy-start = (bf16[768,1536]{1,0:T(8,128)(2,1)S(1)}, bf16[768,1536]{1,0:T(8,128)(2,1)}, u32[]{:S(2)}) copy-start(bf16[768,1536]{1,0:T(8,128)(2,1)} %param.42) | copy-start | bytes 7077892
  7.2 130.4 %all-gather.2.cloned.1.call-start = ((), (), s32[]{:S(2)}) async-start(), calls=%async_computation.4 | async-start | bytes 4718592 | tf_op jit(solution)/shard_map/all_gather | solution.py:166
  7.9 502.3 %reduce-scatter.6.cloned.1.call-start = ((), (), s32[]{:S(2)}) async-start(), calls=%async_computation.5 | async-start | bytes 9437184 | tf_op jit(solution)/shard_map/reduce_scatter | solution.py:231
  8.0 61.7 %collective-permute-start = (bf16[1024,768]{1,0:T(8,128)(2,1)}, bf16[1024,768]{1,0:T(8,128)(2,1)}, u32[]{:S(2)}, u32[]{:S(2)}) collective-permute-start(bf16[1024,768]{1,0:T(8,128)(2,1)} %param.35), channel_id=1, source_target_pairs={{0,1},{1,0},{2,3},{3,2},{4,5},{5,4},{6,7},{7,6},{8,9},{9,8},{10,11... | collective-permute-start | bytes 4718600 | tf_op jit(solution)/shard_map/ppermute | solution.py:18
  13.3 67.1 %copy-start.53 = (f32[768]{0:T(1024)}, f32[768]{0:T(1024)S(1)}, u32[]{:S(2)}) copy-start(f32[768]{0:T(1024)S(1)} %convert_element_type.131) | copy-start | bytes 9220
  14.0 66.5 %copy-start.62 = (f32[768]{0:T(1024)}, f32[768]{0:T(1024)S(1)}, u32[]{:S(2)}) copy-start(f32[768]{0:T(1024)S(1)} %convert_element_type.132) | copy-start | bytes 9220
  15.7 60.0 %copy-start.75 = (bf16[768,1152]{1,0:T(8,128)(2,1)S(1)}, bf16[768,1152]{1,0:T(8,128)(2,1)}, u32[]{:S(2)}) copy-start(bf16[768,1152]{1,0:T(8,128)(2,1)} %param.38) | copy-start | bytes 5308420
  18.0 63.4 %copy-start.27 = (f32[2048,8]{0,1:T(8,128)}, f32[2048,8]{0,1:T(8,128)S(1)}, u32[]{:S(2)}) copy-start(f32[2048,8]{0,1:T(8,128)S(1)} %get-tuple-element.171) | copy-start | bytes 196612
  74.5 6.0 copy-start.14
  74.5 6.0 copy-start.57
  81.5 33.2 %copy-start.10 = (bf16[2048,6,48]{0,2,1:T(8,128)(2,1)}, bf16[2048,6,48]{0,2,1:T(8,128)(2,1)S(1)}, u32[]{:S(2)}) copy-start(bf16[2048,6,48]{0,2,1:T(8,128)(2,1)S(1)} %get-tuple-element.160) | copy-start | bytes 3538948
  83.7 11.7 %copy-start.8 = (bf16[2048,6,64]{0,2,1:T(8,128)(2,1)}, bf16[2048,6,64]{0,2,1:T(8,128)(2,1)S(1)}, u32[]{:S(2)}) copy-start(bf16[2048,6,64]{0,2,1:T(8,128)(2,1)S(1)} %get-tuple-element.196) | copy-start | bytes 4718596
  83.7 11.7 %copy-start.12 = (bf16[2048,6,64]{0,2,1:T(8,128)(2,1)}, bf16[2048,6,64]{0,2,1:T(8,128)(2,1)S(1)}, u32[]{:S(2)}) copy-start(bf16[2048,6,64]{0,2,1:T(8,128)(2,1)S(1)} %get-tuple-element.195) | copy-start | bytes 4718596
  90.1 5.3 copy-start.26
  94.8 9.0 %copy-start.46 = (f32[6,512]{1,0:T(8,128)}, f32[6,512]{1,0:T(8,128)S(1)}, u32[]{:S(2)}) copy-start(f32[6,512]{1,0:T(8,128)S(1)} %fusion.14) | copy-start | bytes 36868
  103.7 9.6 %copy-start.40 = (f32[6,512]{1,0:T(8,128)}, f32[6,512]{1,0:T(8,128)S(1)}, u32[]{:S(2)}) copy-start(f32[6,512]{1,0:T(8,128)S(1)} %get-tuple-element.180) | copy-start | bytes 36868
  126.6 10.9 %copy-start.49 = (f32[6,512]{1,0:T(8,128)}, f32[6,512]{1,0:T(8,128)S(1)}, u32[]{:S(2)}) copy-start(f32[6,512]{1,0:T(8,128)S(1)} %get-tuple-element.176) | copy-start | bytes 36868
  126.6 11.5 %copy-start.33 = (bf16[384,768]{1,0:T(8,128)(2,1)S(1)}, bf16[384,768]{1,0:T(8,128)(2,1)}, u32[]{:S(2)}) copy-start(bf16[384,768]{1,0:T(8,128)(2,1)} %param.40) | copy-start | bytes 1769476
  138.1 8.2 slice-start.8
  151.4 6.4 copy-start.21
  151.4 13.8 %slice-start.5 = ((s8[12582912]{0:T(1024)(128)(4,1)}), s8[4194304]{0:T(1024)(128)(4,1)S(1)}, s32[]{:S(2)}) async-start(s8[12582912]{0:T(1024)(128)(4,1)} %bitcast.102), calls=%async_computation.13 | async-start | bytes 8388608
  151.4 13.8 %slice-start.6 = ((s8[12582912]{0:T(1024)(128)(4,1)}), s8[4194304]{0:T(1024)(128)(4,1)S(1)}, s32[]{:S(2)}) async-start(s8[12582912]{0:T(1024)(128)(4,1)} %bitcast.102), calls=%async_computation.14 | async-start | bytes 8388608
  175.3 6.5 copy-start.9
  206.9 14.0 %copy-start.5 = (f32[2048,6,64]{0,2,1:T(8,128)}, f32[2048,6,64]{0,2,1:T(8,128)S(1)}, u32[]{:S(2)}) copy-start(f32[2048,6,64]{0,2,1:T(8,128)S(1)} %fusion.78) | copy-start | bytes 9437188
  243.6 21.9 %copy-start.11 = (bf16[2048,6,48]{0,2,1:T(8,128)(2,1)S(1)}, bf16[2048,6,48]{0,2,1:T(8,128)(2,1)}, u32[]{:S(2)}) copy-start(bf16[2048,6,48]{0,2,1:T(8,128)(2,1)} %copy-done.10) | copy-start | bytes 3538948
  243.6 21.9 %copy-start.23 = (bf16[2048,6,8]{0,2,1:T(8,128)(2,1)S(1)}, bf16[2048,6,8]{0,2,1:T(8,128)(2,1)}, u32[]{:S(2)}) copy-start(bf16[2048,6,8]{0,2,1:T(8,128)(2,1)} %copy-done.22) | copy-start | bytes 589828
  243.6 21.9 %copy-start.25 = (bf16[2048,6,8]{0,2,1:T(8,128)(2,1)S(1)}, bf16[2048,6,8]{0,2,1:T(8,128)(2,1)}, u32[]{:S(2)}) copy-start(bf16[2048,6,8]{0,2,1:T(8,128)(2,1)} %copy-done.24) | copy-start | bytes 589828
  265.5 8.7 %copy-start.4 = (f32[2048,6,64]{0,2,1:T(8,128)S(1)}, f32[2048,6,64]{0,2,1:T(8,128)}, u32[]{:S(2)}) copy-start(f32[2048,6,64]{0,2,1:T(8,128)} %copy-done.3) | copy-start | bytes 9437188
  274.2 7.2 copy-start.17
  274.2 7.2 copy-start.18
  274.2 7.2 copy-start.28
  274.2 7.2 copy-start.30
  308.4 201.8 %reduce-scatter.8.cloned.1.call-start = ((), (), s32[]{:S(2)}) async-start(), calls=%async_computation.6 | async-start | bytes 9437184 | tf_op jit(solution)/shard_map/reduce_scatter | solution.py:232
  309.1 36.0 %copy-start.55 = (f32[768]{0:T(1024)}, f32[768]{0:T(1024)S(1)}, u32[]{:S(2)}) copy-start(f32[768]{0:T(1024)S(1)} %convert_element_type.142) | copy-start | bytes 9220
  309.1 36.0 %copy-start.64 = (f32[768]{0:T(1024)}, f32[768]{0:T(1024)S(1)}, u32[]{:S(2)}) copy-start(f32[768]{0:T(1024)S(1)} %convert_element_type.143) | copy-start | bytes 9220
  309.1 35.9 %copy-start.71 = (bf16[2048,768]{1,0:T(8,128)(2,1)S(1)}, bf16[2048,768]{1,0:T(8,128)(2,1)}, u32[]{:S(2)}) copy-start(bf16[2048,768]{1,0:T(8,128)(2,1)} %all-gather.2.cloned.1.call-done) | copy-start | bytes 9437188
  309.1 35.9 %copy-start.73 = (bf16[1536,768]{1,0:T(8,128)(2,1)S(1)}, bf16[1536,768]{1,0:T(8,128)(2,1)}, u32[]{:S(2)}) copy-start(bf16[1536,768]{1,0:T(8,128)(2,1)} %param.44) | copy-start | bytes 7077892
  372.0 174.7 %reduce-scatter.4.cloned.1.call-start = ((), (), s32[]{:S(2)}) async-start(), calls=%async_computation.3 | async-start | bytes 9437184 | tf_op jit(solution)/shard_map/reduce_scatter | solution.py:159
  372.7 11.0 %slice-start = ((s8[18874368]{0:T(1024)(128)(4,1)}), s8[4194304]{0:T(1024)(128)(4,1)S(1)}, s32[]{:S(2)}) async-start(s8[18874368]{0:T(1024)(128)(4,1)} %bitcast.100), calls=%async_computation.8 | async-start | bytes 8388608
  372.7 11.0 %slice-start.1 = ((s8[18874368]{0:T(1024)(128)(4,1)}), s8[4194304]{0:T(1024)(128)(4,1)S(1)}, s32[]{:S(2)}) async-start(s8[18874368]{0:T(1024)(128)(4,1)} %bitcast.100), calls=%async_computation.9 | async-start | bytes 8388608
  377.0 6.7 slice-start.2
  377.0 7.7 slice-start.3
  377.0 8.3 slice-start.4
  377.0 8.2 copy-start.41
  377.0 8.2 copy-start.48
  385.3 5.5 copy-start.50
  385.3 5.5 copy-start.52
  390.8 12.4 %copy-start.74 = (bf16[1536,768]{1,0:T(8,128)(2,1)S(1)}, bf16[1536,768]{1,0:T(8,128)(2,1)}, u32[]{:S(2)}) copy-start(bf16[1536,768]{1,0:T(8,128)(2,1)} %param.44) | copy-start | bytes 7077892
  403.1 7.7 copy-start.16
  403.1 7.7 copy-start.34
  415.4 5.4 copy-start.54
  415.4 5.4 copy-start.63
  415.4 397.2 %all-reduce.7.cloned.1.call-start = ((), (), s32[]{:S(2)}) async-start(), calls=%async_computation.7 | async-start | bytes 28311552 | tf_op jit(solution)/shard_map/psum | solution.py:227
  415.5 5.3 copy-start.15
  415.5 15.0 %slice-start.14 = ((s8[6291456]{0:T(1024)(128)(4,1)}), s8[4194304]{0:T(1024)(128)(4,1)S(1)}, s32[]{:S(2)}) async-start(s8[6291456]{0:T(1024)(128)(4,1)} %bitcast.125), calls=%async_computation.22 | async-start | bytes 8388608
  415.5 22.2 %slice-start.16 = ((s8[6291456]{0:T(1024)(128)(4,1)}), s8[4194304]{0:T(1024)(128)(4,1)S(1)}, s32[]{:S(2)}) async-start(s8[6291456]{0:T(1024)(128)(4,1)} %bitcast.127), calls=%async_computation.24 | async-start | bytes 8388608
  420.8 9.7 %copy-start.72 = (bf16[2048,768]{1,0:T(8,128)(2,1)S(1)}, bf16[2048,768]{1,0:T(8,128)(2,1)}, u32[]{:S(2)}) copy-start(bf16[2048,768]{1,0:T(8,128)(2,1)} %all-gather.2.cloned.1.call-done) | copy-start | bytes 9437188
  420.8 9.7 %slice-start.15 = ((s8[6291456]{0:T(1024)(128)(4,1)}), s8[2097152]{0:T(1024)(128)(4,1)S(1)}, s32[]{:S(2)}) async-start(s8[6291456]{0:T(1024)(128)(4,1)} %bitcast.125), calls=%async_computation.23 | async-start | bytes 4194304
  420.8 16.9 %slice-start.17 = ((s8[6291456]{0:T(1024)(128)(4,1)}), s8[2097152]{0:T(1024)(128)(4,1)S(1)}, s32[]{:S(2)}) async-start(s8[6291456]{0:T(1024)(128)(4,1)} %bitcast.127), calls=%async_computation.25 | async-start | bytes 4194304
  430.5 7.2 copy-start.56
  430.5 7.2 copy-start.65
  595.4 225.6 %copy-start.66 = (f32[768]{0:T(1024)}, f32[768]{0:T(1024)S(1)}, u32[]{:S(2)}) copy-start(f32[768]{0:T(1024)S(1)} %get-tuple-element.231) | copy-start | bytes 9220
  812.6 5.9 slice-start.12
  813.2 5.3 slice-start.13
  (36 other events, 104.7 us)
Sparse Core Ops, SparseCore 0:
  9.6 69.9 all-gather.1
  308.5 79.3 reduce-scatter.5
  390.4 77.0 reduce-scatter.7
  469.6 77.0 reduce-scatter.3
  552.9 259.6 all-reduce.6
